TPU v7x, 32 devices: a whole 2x2x4 slice. The times are simulated.
32 devices in a mesh: gx: 2 (over y), gy: 4 (over z), gz: 4 (over x, core).
Axes of the slice: x: 2, y: 2, z: 4, core: 2. Of those that a mesh axis runs over, the one named last changes fastest.
Arguments:
- field: float32 [4, 512, 16, 512], P('gx', 'gy', None, 'gz'), may hold values from -45 to 45
- start_basis: float32 [512, 128], replicated, may hold values from -6 to 6
Outputs:
- factor_out: float32 [512, 512], P('gy', 'gz')
- core: float32 [4, 128, 16, 512], P('gx', 'gy', None, 'gz')
All inputs are finite; a program needn't handle non-finite values.
Results may differ from a plain program's by a relative error of at most 0.0003.
Values sent between devices are 32-bit elements; how exact they have to be, the bound alone decides.
A program may use at most 64 MiB of HBM per device.

v0:
```python
import functools

import jax
import jax.numpy as jnp
from jax import lax
from jax.experimental import pallas as pl
from jax.experimental.pallas import tpu as pltpu
from jax.sharding import PartitionSpec as P

ITERS = 2
B = 128
MESH = pl.DeviceIdType.MESH
VMEM = pl.BlockSpec(memory_space=pltpu.VMEM)
ANY = pl.BlockSpec(memory_space=pl.ANY)
F32 = jnp.float32
BF16 = jnp.bfloat16


def pieces(a):
    hi = a.astype(BF16)
    return hi, (a - hi.astype(F32)).astype(BF16)


def dot3(a, b, ca, cb):
    ah, al = pieces(a)
    bh, bl = pieces(b)
    return lax.dot_general(
        jnp.concatenate([ah, ah, al], axis=ca),
        jnp.concatenate([bh, bl, bh], axis=cb),
        (((ca,), (cb,)), ((), ())),
        preferred_element_type=F32,
    )


def upper(nb):
    return [(i, j) for i in range(nb) for j in range(i, nb)]


def gram_kernel(sizes, field, full, reg, part, gram, tmp_c, tmp_x, tmp_g, tmp_y, sems, ssem, rsem, lsem):
    n_gx, n_gy, n_gz = sizes
    gx, gy, gz = (lax.axis_index(a) for a in ("gx", "gy", "gz"))
    planes, rows = field.shape[0], field.shape[1]
    quarter = field.shape[2] // n_gy
    chunks = planes * quarter
    nb = gram.shape[0] // B

    def peer(axis, index):
        where = {"gx": gx, "gy": gy, "gz": gz}
        where[axis] = index
        return (where["gx"], where["gy"], where["gz"])

    core = lax.rem(gz, 2)
    other_core = gz + 1 - 2 * core
    half = lax.div(gz, 2)
    other_half = gz + 2 - 4 * half
    y_peers = [lax.rem(gy + k, n_gy) for k in range(1, n_gy)]
    x_peers = [lax.rem(gx + k, n_gx) for k in range(1, n_gx)]
    greet = [peer("gy", d) for d in y_peers] + [peer("gx", d) for d in x_peers]
    greet += [peer("gz", other_core), peer("gz", other_half)]
    barrier = pltpu.get_barrier_semaphore()
    for who in greet:
        pl.semaphore_signal(barrier, inc=1, device_id=who, device_id_type=MESH)
    pl.semaphore_wait(barrier, len(greet))

    mine = pl.ds(pl.multiple_of(gy * rows, rows), rows)

    def send(c, k):
        x, s = c // quarter, c % quarter
        d = y_peers[k]
        return pltpu.make_async_remote_copy(
            src_ref=field.at[x, :, d * quarter + s, :],
            dst_ref=reg.at[c, mine, :],
            send_sem=ssem.at[c, k],
            recv_sem=rsem.at[c, k],
            device_id=peer("gy", d),
            device_id_type=MESH,
        )

    def keep(c):
        x, s = c // quarter, c % quarter
        return pltpu.make_async_copy(
            field.at[x, :, gy * quarter + s, :], reg.at[c, mine, :], lsem.at[c]
        )

    @pl.loop(0, chunks)
    def _(c):
        for k in range(n_gy - 1):
            send(c, k).start()
        keep(c).start()

    gram[...] = jnp.zeros_like(gram)

    @pl.loop(0, chunks)
    def _(c):
        for k in range(n_gy - 1):
            send(c, k).wait()
        keep(c).wait()
        f = reg[c]
        gram[...] += dot3(f, f, 1, 1)

    for b, (i, j) in enumerate(upper(nb)):
        part[b * B:(b + 1) * B, :] = gram[i * B:(i + 1) * B, j * B:(j + 1) * B]

    def swap(src, dst, s, who):
        return pltpu.make_async_remote_copy(
            src_ref=src, dst_ref=dst, send_sem=sems.at[0, s], recv_sem=sems.at[1, s],
            device_id=who, device_id_type=MESH,
        )

    def span(start, size):
        return pl.ds(pl.multiple_of(start, 8), size)

    total = part.shape[0]
    s = 0
    n_c = total // 2
    keep_c = core * n_c
    cp = swap(part.at[span(n_c - keep_c, n_c), :], tmp_c, s, peer("gz", other_core))
    cp.start()
    cp.wait()
    s += 1
    part[span(keep_c, n_c), :] += tmp_c[...]
    n_x = n_c // 2
    keep_x = keep_c + half * n_x
    cp = swap(part.at[span(keep_c + n_x - half * n_x, n_x), :], tmp_x, s, peer("gz", other_half))
    cp.start()
    cp.wait()
    s += 1
    part[span(keep_x, n_x), :] += tmp_x[...]
    n_g = n_x // n_gx
    keep_g = keep_x + gx * n_g
    cps = []
    for k, d in enumerate(x_peers):
        cp = swap(part.at[span(keep_x + d * n_g, n_g), :], tmp_g.at[k], s, peer("gx", d))
        cp.start()
        cps.append(cp)
        s += 1
    for cp in cps:
        cp.wait()
    acc = part[span(keep_g, n_g), :]
    for k in range(n_gx - 1):
        acc += tmp_g[k]
    part[span(keep_g, n_g), :] = acc
    cps = []
    for k, d in enumerate(y_peers):
        cp = swap(part.at[span(keep_g, n_g), :], tmp_y.at[k], s, peer("gy", d))
        cp.start()
        cps.append(cp)
        s += 1
    for cp in cps:
        cp.wait()
    acc = part[span(keep_g, n_g), :]
    for k in range(n_gy - 1):
        acc += tmp_y[k]
    full[span(keep_g, n_g), :] = acc
    cps = []
    for k, d in enumerate(x_peers):
        here = full.at[span(keep_g, n_g), :]
        cp = swap(here, here, s, peer("gx", d))
        cp.start()
        cps.append(cp)
        s += 1
    for cp in cps:
        cp.wait()
    here = full.at[span(keep_x, n_x), :]
    cp = swap(here, here, s, peer("gz", other_half))
    cp.start()
    cp.wait()
    s += 1
    here = full.at[span(keep_c, n_c), :]
    cp = swap(here, here, s, peer("gz", other_core))
    cp.start()
    cp.wait()


def factor_blocks(refs):
    sub = lax.broadcasted_iota(jnp.int32, (8, B), 0)
    for p in range(B // 8):
        lo = 8 * p
        for ref in refs:
            a = ref[lo:lo + 8, :B]
            e = ref[lo:lo + 8, B:]
            cols = [jnp.broadcast_to(a[:, lo + k:lo + k + 1], (8, B)) for k in range(8)]
            for j in range(8):
                r = lax.rsqrt(cols[j][j:j + 1])
                coef = jnp.where(sub > j, cols[j] * r, 0.0)
                ua, ue = a[j:j + 1] * r, e[j:j + 1] * r
                a = jnp.where(sub == j, ua, a - coef * ua)
                e = jnp.where(sub == j, ue, e - coef * ue)
                for k in range(j + 1, 8):
                    cols[k] = cols[k] - coef * (cols[k][j:j + 1] * r)
            ref[lo:lo + 8, :B] = a
            ref[lo:lo + 8, B:] = e
            if lo + 8 < B:
                u = jnp.concatenate([a, e], axis=1)
                ah = a.astype(BF16).astype(F32)
                al = a - ah
                uh = u.astype(BF16).astype(F32)
                ul = u - uh
                lhs = jnp.concatenate([ah, ah, al, al], axis=0).astype(BF16)
                rhs = jnp.concatenate([uh, ul, uh, ul], axis=0).astype(BF16)
                down = lax.dot_general(
                    lhs, rhs, (((0,), (0,)), ((), ())), preferred_element_type=F32
                )
                ref[lo + 8:, :] -= down[lo + 8:]


def solve_kernel(columns, packed, start, factor, basis_t, g, r, m_g, m_s):
    n = g.shape[0]
    nb = n // B
    row = lax.broadcasted_iota(jnp.int32, (B, B), 0)
    col = lax.broadcasted_iota(jnp.int32, (B, B), 1)
    eye = jnp.where(row == col, 1.0, 0.0).astype(F32)
    for b, (i, j) in enumerate(upper(nb)):
        block = packed[b * B:(b + 1) * B, :]
        g[i * B:(i + 1) * B, j * B:(j + 1) * B] = block
        if i != j:
            g[j * B:(j + 1) * B, i * B:(i + 1) * B] = block.T
        r[i * B:(i + 1) * B, j * B:(j + 1) * B] = block
    basis_t[...] = start[...].T
    for step in range(max(nb, ITERS)):
        refs = []
        if step < nb:
            lo, hi = step * B, (step + 1) * B
            m_g[:, :B] = r[lo:hi, lo:hi]
            m_g[:, B:] = eye
            refs.append(m_g)
        if step < ITERS:
            wide_t = dot3(basis_t[...], g[...], 1, 0)
            m_s[:, :B] = dot3(wide_t, wide_t, 1, 1)
            m_s[:, B:] = eye
            refs.append(m_s)
        factor_blocks(refs)
        if step < ITERS:
            basis_t[...] = dot3(jnp.where(row >= col, m_s[:, B:], 0.0), wide_t, 1, 0)
        if step < nb:
            r[lo:hi, lo:hi] = jnp.where(row <= col, m_g[:, :B], 0.0)
            if step + 1 < nb:
                u = dot3(jnp.where(row >= col, m_g[:, B:], 0.0), r[lo:hi, hi:], 1, 0)
                r[lo:hi, hi:] = u
                r[hi:, hi:] -= dot3(u, u, 0, 0)
    gy, gz = lax.axis_index("gy"), lax.axis_index("gz")
    scale = 1.0 / jnp.sqrt(F32(columns))
    factor[...] = jnp.zeros_like(factor)
    for i, j in upper(nb):
        @pl.when((gy == j) & (gz == i))
        def _():
            factor[...] = r[i * B:(i + 1) * B, j * B:(j + 1) * B].T * scale


def core_kernel(n_gy, basis_t, reg, core, proj, ssem, rsem, lsem):
    gx, gy, gz = (lax.axis_index(a) for a in ("gx", "gy", "gz"))
    peers = [lax.rem(gy + k, n_gy) for k in range(1, n_gy)]
    barrier = pltpu.get_barrier_semaphore()
    for d in peers:
        pl.semaphore_signal(barrier, inc=1, device_id=(gx, d, gz), device_id_type=MESH)
    planes, kept = core.shape[0], core.shape[2]
    quarter = core.shape[1] // n_gy
    mine = pl.ds(gy * quarter, quarter)
    bh, bl = pieces(basis_t[...])
    left = jnp.concatenate([bh, bh, bl], axis=1)
    cps = []
    for x in range(planes):
        for s in range(quarter):
            fh, fl = pieces(reg[x * quarter + s])
            res = jnp.dot(left, jnp.concatenate([fh, fl, fh], axis=0), preferred_element_type=F32)
            for d in range(n_gy):
                proj[d, x, s] = res[d * kept:(d + 1) * kept]
        if x == 0:
            pl.semaphore_wait(barrier, n_gy - 1)
        for k, d in enumerate(peers):
            cp = pltpu.make_async_remote_copy(
                src_ref=proj.at[d, x], dst_ref=core.at[x, mine], send_sem=ssem.at[x, k],
                recv_sem=rsem.at[x, k], device_id=(gx, d, gz), device_id_type=MESH,
            )
            cp.start()
            cps.append(cp)
        cp = pltpu.make_async_copy(proj.at[gy, x], core.at[x, mine], lsem.at[x])
        cp.start()
        cps.append(cp)
    for cp in cps:
        cp.wait()


def per_device(sizes, field, start_basis):
    n_gx, n_gy, n_gz = sizes
    planes, rows, species, width = field.shape
    n, rank = start_basis.shape
    quarter = species // n_gy
    chunks = planes * quarter
    nb = n // B
    total = len(upper(nb)) * B
    columns = planes * n_gx * species * width * n_gz
    n_g = total // 4 // n_gx
    n_sems = 2 + 2 * (n_gx - 1) + (n_gy - 1) + 2
    packed, reg = pl.pallas_call(
        functools.partial(gram_kernel, sizes),
        out_shape=(
            jax.ShapeDtypeStruct((total, B), F32),
            jax.ShapeDtypeStruct((chunks, n, width), F32),
        ),
        in_specs=[ANY],
        out_specs=(VMEM, VMEM),
        scratch_shapes=[
            pltpu.VMEM((total, B), F32),
            pltpu.VMEM((n, n), F32),
            pltpu.VMEM((total // 2, B), F32),
            pltpu.VMEM((total // 4, B), F32),
            pltpu.VMEM((max(n_gx - 1, 1), n_g, B), F32),
            pltpu.VMEM((n_gy - 1, n_g, B), F32),
            pltpu.SemaphoreType.DMA((2, n_sems)),
            pltpu.SemaphoreType.DMA((chunks, n_gy - 1)),
            pltpu.SemaphoreType.DMA((chunks, n_gy - 1)),
            pltpu.SemaphoreType.DMA((chunks,)),
        ],
        compiler_params=pltpu.CompilerParams(
            collective_id=0, has_side_effects=True, vmem_limit_bytes=32 << 20
        ),
        name="gram",
    )(field)
    factor, basis_t = pl.pallas_call(
        functools.partial(solve_kernel, columns),
        out_shape=(
            jax.ShapeDtypeStruct((n // n_gy, n // n_gz), F32),
            jax.ShapeDtypeStruct((rank, n), F32),
        ),
        in_specs=[VMEM, VMEM],
        out_specs=(VMEM, VMEM),
        scratch_shapes=[
            pltpu.VMEM((n, n), F32),
            pltpu.VMEM((n, n), F32),
            pltpu.VMEM((B, 2 * B), F32),
            pltpu.VMEM((B, 2 * B), F32),
        ],
        compiler_params=pltpu.CompilerParams(vmem_limit_bytes=32 << 20),
        name="solve",
    )(packed, start_basis)
    core = pl.pallas_call(
        functools.partial(core_kernel, n_gy),
        out_shape=jax.ShapeDtypeStruct((planes, species, rank // n_gy, width), F32),
        in_specs=[VMEM, VMEM],
        out_specs=VMEM,
        scratch_shapes=[
            pltpu.VMEM((n_gy, planes, quarter, rank // n_gy, width), F32),
            pltpu.SemaphoreType.DMA((planes, n_gy - 1)),
            pltpu.SemaphoreType.DMA((planes, n_gy - 1)),
            pltpu.SemaphoreType.DMA((planes,)),
        ],
        compiler_params=pltpu.CompilerParams(
            collective_id=1, has_side_effects=True, vmem_limit_bytes=32 << 20
        ),
        name="core",
    )(basis_t, reg)
    return factor, jnp.transpose(core, (0, 2, 1, 3))


def solution(mesh):
    sizes = tuple(mesh.shape[a] for a in ("gx", "gy", "gz"))
    return jax.shard_map(
        functools.partial(per_device, sizes),
        mesh=mesh,
        in_specs=(P("gx", "gy", None, "gz"), P()),
        out_specs=(P("gy", "gz"), P("gx", "gy", None, "gz")),
        check_vma=False,
    )
```

profile of v0, /device:TPU:0, one launch (start us, length us, event | category | flops | bytes accessed | tf_op | source)
XLA Modules:
  0.0 121.2 jit_solution(6061828227446735240)
XLA Ops:
  0.6 0.0 copy-start
  0.6 1.6 %copy-done = f32[2,128,16,128]{3,2,1,0:T(8,128)S(1)} copy-done((f32[2,128,16,128]{3,2,1,0:T(8,128)S(1)}, f32[2,128,16,128]{3,2,1,0:T(8,128)}, u32[]{:S(2)}) %copy-start) | copy-done | bytes 2097176
  2.2 0.0 copy-start.1
  2.2 78.3 %gram.1 = (f32[1280,128]{1,0:T(8,128)S(1)}, f32[8,512,128]{2,1,0:T(8,128)S(1)}) custom-call(f32[2,128,16,128]{3,2,1,0:T(8,128)S(1)} %copy-done), custom_call_target="tpu_custom_call" | custom-call | tf_op jit(solution)/shard_map/gram/pallas_call | solution.py:295
  80.6 0.0 copy-done.1
  80.6 24.6 %solve.1 = (f32[128,128]{1,0:T(8,128)}, f32[128,512]{1,0:T(8,128)S(1)}) custom-call(f32[1280,128]{1,0:T(8,128)S(1)} %get-tuple-element.6.packed, f32[512,128]{1,0:T(8,128)S(1)} %copy-done.1), custom_call_target="tpu_custom_call" | custom-call | tf_op jit(solution)/shard_map/solve/pallas_call | solution.py:320
  105.2 14.9 %core.1 = f32[2,16,32,128]{3,2,1,0:T(8,128)S(1)} custom-call(f32[128,512]{1,0:T(8,128)S(1)} %get-tuple-element.8.basis_t, f32[8,512,128]{2,1,0:T(8,128)S(1)} %get-tuple-element.9.reg), custom_call_target="tpu_custom_call" | custom-call | tf_op jit(solution)/shard_map/core/pallas_call | solution.py:337
  120.1 1.1 copy.4
Async XLA Ops:
  0.6 1.6 %copy-start = (f32[2,128,16,128]{3,2,1,0:T(8,128)S(1)}, f32[2,128,16,128]{3,2,1,0:T(8,128)}, u32[]{:S(2)}) copy-start(f32[2,128,16,128]{3,2,1,0:T(8,128)} %field.1) | copy-start | bytes 6291460
  2.2 78.4 %copy-start.1 = (f32[512,128]{1,0:T(8,128)S(1)}, f32[512,128]{1,0:T(8,128)}, u32[]{:S(2)}) copy-start(f32[512,128]{1,0:T(8,128)} %start.1) | copy-start | bytes 786436
where the time goes:
time: 121 us
  Pallas kernels  118 us (98%)
  local copies, waits for them, and re-layouts  2.69 us (2%)
    pallas_call x1, Pallas kernels, per_device(): pl.pallas_call(functools.partial(gram_kernel, sizes), out_shape=(jax.Shap...  78.3 us
    pallas_call x1, Pallas kernels, per_device(): pl.pallas_call(functools.partial(solve_kernel, columns), out_shape=(jax.S...  24.6 us
    pallas_call x1, Pallas kernels, per_device(): pl.pallas_call(functools.partial(core_kernel, n_gy), out_shape=jax.ShapeD...  14.9 us
    unnamed x5, local copies, waits for them, and re-layouts  2.69 us

commit v1 on v0

v1 whole, which is shorter than its diff:
```python
import functools

import jax
import jax.numpy as jnp
from jax import lax
from jax.experimental import pallas as pl
from jax.experimental.pallas import tpu as pltpu
from jax.sharding import PartitionSpec as P

ITERS = 2
B = 128
MESH = pl.DeviceIdType.MESH
VMEM = pl.BlockSpec(memory_space=pltpu.VMEM)
HBM = pl.BlockSpec(memory_space=pltpu.HBM)
F32 = jnp.float32
BF16 = jnp.bfloat16


def pieces(a):
    hi = a.astype(BF16)
    return hi, (a - hi.astype(F32)).astype(BF16)


def dot3(a, b, ca, cb):
    ah, al = pieces(a)
    bh, bl = pieces(b)
    return lax.dot_general(
        jnp.concatenate([ah, ah, al], axis=ca),
        jnp.concatenate([bh, bl, bh], axis=cb),
        (((ca,), (cb,)), ((), ())),
        preferred_element_type=F32,
    )


def above(nb):
    return [(i, j) for i in range(nb) for j in range(i + 1, nb)]


def upper(nb):
    return [(i, j) for i in range(nb) for j in range(i, nb)]


def gram_kernel(
    sizes, field, full, full_d, reg, part, gram, tmp_c, tmp_g, tmp_y,
    own, diag, part_d, tmp_dc, tmp_dg, sems, ssem, rsem, lsem, osem,
):
    n_gx, n_gy, n_gz = sizes
    gx, gy, gz = (lax.axis_index(a) for a in ("gx", "gy", "gz"))
    planes, rows = field.shape[0], field.shape[1]
    quarter = field.shape[2] // n_gy
    chunks = planes * quarter
    nb = gram.shape[0] // B

    def peer(axis, index):
        where = {"gx": gx, "gy": gy, "gz": gz}
        where[axis] = index
        return (where["gx"], where["gy"], where["gz"])

    core = lax.rem(gz, 2)
    other_core = gz + 1 - 2 * core
    half = lax.div(gz, 2)
    y_peers = [lax.rem(gy + k, n_gy) for k in range(1, n_gy)]
    offsets = [(dx, dg) for dx in range(2) for dg in range(n_gx) if dx or dg]
    plane = []
    for dx, dg in offsets:
        h, g = lax.rem(half + dx, 2), lax.rem(gx + dg, n_gx)
        plane.append((h, g, (g, gy, 2 * h + core)))
    greet = [peer("gy", d) for d in y_peers] + [who for _, _, who in plane]
    greet.append(peer("gz", other_core))
    barrier = pltpu.get_barrier_semaphore()
    for who in greet:
        pl.semaphore_signal(barrier, inc=1, device_id=who, device_id_type=MESH)
    pl.semaphore_wait(barrier, len(greet))

    mine = pl.ds(pl.multiple_of(gy * rows, rows), rows)

    def send(c, k):
        x, s = c // quarter, c % quarter
        d = y_peers[k]
        return pltpu.make_async_remote_copy(
            src_ref=field.at[x, :, d * quarter + s, :],
            dst_ref=reg.at[c, mine, :],
            send_sem=ssem.at[c, k],
            recv_sem=rsem.at[c, k],
            device_id=peer("gy", d),
            device_id_type=MESH,
        )

    def keep(c):
        x, s = c // quarter, c % quarter
        return pltpu.make_async_copy(
            field.at[x, :, gy * quarter + s, :], reg.at[c, mine, :], lsem.at[c]
        )

    @pl.loop(0, chunks)
    def _(c):
        for k in range(n_gy - 1):
            send(c, k).start()
        keep(c).start()

    def keep_own(q):
        species = field.shape[2]
        return pltpu.make_async_copy(
            field.at[q // species, :, q % species, :], own.at[q], osem.at[q]
        )

    @pl.loop(0, own.shape[0])
    def _(q):
        keep_own(q).start()

    used = [0]

    def swap(src, dst, who):
        s = used[0]
        used[0] += 1
        cp = pltpu.make_async_remote_copy(
            src_ref=src, dst_ref=dst, send_sem=sems.at[0, s], recv_sem=sems.at[1, s],
            device_id=who, device_id_type=MESH,
        )
        cp.start()
        return cp

    def span(start, size):
        return pl.ds(pl.multiple_of(start, 8), size)

    partner = peer("gz", other_core)

    diag[...] = jnp.zeros_like(diag)

    @pl.loop(0, own.shape[0])
    def _(q):
        keep_own(q).wait()
        f = own[q]
        diag[...] += dot3(f, f, 1, 1)

    n_p = 2 * n_gx
    rows_d = part_d.shape[1]
    for p in range(2 * n_p):
        part_d[p] = diag[p * rows_d:(p + 1) * rows_d]
    cp = swap(part_d.at[pl.ds((1 - core) * n_p, n_p)], tmp_dc, partner)
    cp.wait()
    for p in range(n_p):
        part_d[core * n_p + p] += tmp_dc[p]
    cps = []
    for k, (h, g, who) in enumerate(plane):
        cps.append(swap(part_d.at[core * n_p + h * n_gx + g], tmp_dg.at[k], who))
    for cp in cps:
        cp.wait()
    mine_d = core * n_p + half * n_gx + gx
    acc = part_d[mine_d]
    for k in range(len(plane)):
        acc += tmp_dg[k]
    full_d[gy, mine_d] = acc
    diag_cps = []
    for d in y_peers:
        here = full_d.at[gy, mine_d]
        diag_cps.append(swap(here, here, peer("gy", d)))

    gram[...] = jnp.zeros_like(gram)

    @pl.loop(0, chunks)
    def _(c):
        for k in range(n_gy - 1):
            send(c, k).wait()
        keep(c).wait()
        f = reg[c]
        gram[...] += dot3(f, f, 1, 1)

    for b, (i, j) in enumerate(above(nb)):
        part[b * B:(b + 1) * B, :] = gram[i * B:(i + 1) * B, j * B:(j + 1) * B]

    total = part.shape[0]
    n_c = total // 2
    keep_c = core * n_c
    cp = swap(part.at[span(n_c - keep_c, n_c), :], tmp_c, partner)
    cp.wait()
    part[span(keep_c, n_c), :] += tmp_c[...]
    n_g = n_c // n_p

    def piece(h, g):
        return span(keep_c + (h * n_gx + g) * n_g, n_g)

    mine_g = piece(half, gx)
    cps = []
    for k, (h, g, who) in enumerate(plane):
        cps.append(swap(part.at[piece(h, g), :], tmp_g.at[k], who))
    for cp in diag_cps:
        cp.wait()
    for cp in cps:
        cp.wait()
    acc = part[mine_g, :]
    for k in range(len(plane)):
        acc += tmp_g[k]
    part[mine_g, :] = acc
    cps = []
    for k, d in enumerate(y_peers):
        cps.append(swap(part.at[mine_g, :], tmp_y.at[k], peer("gy", d)))
    here = full_d.at[:, mine_d]
    plane_d = [swap(here, here, who) for _, _, who in plane]
    onward = [swap(here, here, partner)]
    came_from = []
    for dx, dg in offsets:
        h = lax.rem(half + 2 - dx, 2)
        g = lax.rem(gx + n_gx - dg, n_gx)
        came_from.append((h, g))
    for cp, (h, g) in zip(plane_d, came_from):
        cp.wait_recv()
        here = full_d.at[:, core * n_p + h * n_gx + g]
        onward.append(swap(here, here, partner))
    for cp in cps:
        cp.wait()
    acc = part[mine_g, :]
    for k in range(n_gy - 1):
        acc += tmp_y[k]
    full[mine_g, :] = acc
    here = full.at[mine_g, :]
    cps = [swap(here, here, who) for _, _, who in plane]
    onward.append(swap(here, here, partner))
    for cp, (h, g) in zip(cps, came_from):
        cp.wait_recv()
        here = full.at[piece(h, g), :]
        onward.append(swap(here, here, partner))
    for cp in plane_d + cps:
        cp.wait_send()
    for cp in onward:
        cp.wait()


PANEL = 16


def factor_blocks(refs):
    sub = lax.broadcasted_iota(jnp.int32, (PANEL, B), 0)
    for lo in range(0, B, PANEL):
        for ref in refs:
            a = ref[lo:lo + PANEL, :B]
            e = ref[lo:lo + PANEL, B:]
            cols = [jnp.broadcast_to(a[:, lo + k:lo + k + 1], (PANEL, B)) for k in range(PANEL)]
            for j in range(PANEL):
                r = lax.rsqrt(cols[j][j:j + 1])
                coef = jnp.where(sub > j, cols[j] * r, 0.0)
                ua, ue = a[j:j + 1] * r, e[j:j + 1] * r
                a = jnp.where(sub == j, ua, a - coef * ua)
                e = jnp.where(sub == j, ue, e - coef * ue)
                for k in range(j + 1, PANEL):
                    cols[k] = cols[k] - coef * (cols[k][j:j + 1] * r)
            ref[lo:lo + PANEL, :B] = a
            ref[lo:lo + PANEL, B:] = e
            if lo + PANEL < B:
                u = jnp.concatenate([a, e], axis=1)
                ah = a.astype(BF16).astype(F32)
                al = a - ah
                uh = u.astype(BF16).astype(F32)
                ul = u - uh
                lhs = jnp.concatenate([ah, ah, al, al], axis=0).astype(BF16)
                rhs = jnp.concatenate([uh, ul, uh, ul], axis=0).astype(BF16)
                down = lax.dot_general(
                    lhs, rhs, (((0,), (0,)), ((), ())), preferred_element_type=F32
                )
                ref[lo + PANEL:, :] -= down[lo + PANEL:]


def triangles():
    row = lax.broadcasted_iota(jnp.int32, (B, B), 0)
    col = lax.broadcasted_iota(jnp.int32, (B, B), 1)
    return row, col, jnp.where(row == col, 1.0, 0.0).astype(F32)


def load_block(step, r, m_g, eye):
    lo, hi = step * B, (step + 1) * B
    m_g[:, :B] = r[lo:hi, lo:hi]
    m_g[:, B:] = eye


def finish_block(step, r, m_g, row, col):
    lo, hi = step * B, (step + 1) * B
    r[lo:hi, lo:hi] = jnp.where(row <= col, m_g[:, :B], 0.0)
    if hi < r.shape[0]:
        u = dot3(jnp.where(row >= col, m_g[:, B:], 0.0), r[lo:hi, hi:], 1, 0)
        r[lo:hi, hi:] = u
        r[hi:, hi:] -= dot3(u, u, 0, 0)


def basis_kernel(packed, diagonal, start, basis_t, r, g, m_g, m_s):
    nb = r.shape[0] // B
    row, col, eye = triangles()
    for b, (i, j) in enumerate(above(nb)):
        block = packed[b * B:(b + 1) * B, :]
        g[i * B:(i + 1) * B, j * B:(j + 1) * B] = block
        g[j * B:(j + 1) * B, i * B:(i + 1) * B] = block.T
        r[i * B:(i + 1) * B, j * B:(j + 1) * B] = block
        r[j * B:(j + 1) * B, i * B:(i + 1) * B] = jnp.zeros_like(block)
    rows = diagonal.shape[2]
    for i in range(nb):
        for p in range(B // rows):
            there = slice(i * B + p * rows, i * B + (p + 1) * rows)
            g[there, i * B:(i + 1) * B] = diagonal[i, p]
            r[there, i * B:(i + 1) * B] = diagonal[i, p]
    basis_t[...] = start[...].T
    for step in range(ITERS):
        load_block(step, r, m_g, eye)
        wide_t = dot3(basis_t[...], g[...], 1, 0)
        m_s[:, :B] = dot3(wide_t, wide_t, 1, 1)
        m_s[:, B:] = eye
        factor_blocks([m_s, m_g])
        basis_t[...] = dot3(jnp.where(row >= col, m_s[:, B:], 0.0), wide_t, 1, 0)
        finish_block(step, r, m_g, row, col)


def core_kernel(n_gy, columns, basis_t, reg, started, core, factor, r, m_g, proj, ssem, rsem, lsem):
    gx, gy, gz = (lax.axis_index(a) for a in ("gx", "gy", "gz"))
    peers = [lax.rem(gy + k, n_gy) for k in range(1, n_gy)]
    barrier = pltpu.get_barrier_semaphore()
    for d in peers:
        pl.semaphore_signal(barrier, inc=1, device_id=(gx, d, gz), device_id_type=MESH)
    planes, kept = core.shape[0], core.shape[2]
    quarter = core.shape[1] // n_gy
    mine = pl.ds(gy * quarter, quarter)
    bh, bl = pieces(basis_t[...])
    left = jnp.concatenate([bh, bh, bl], axis=1)
    cps = []
    for x in range(planes):
        for s in range(quarter):
            fh, fl = pieces(reg[x * quarter + s])
            res = jnp.dot(left, jnp.concatenate([fh, fl, fh], axis=0), preferred_element_type=F32)
            for d in range(n_gy):
                proj[d, x, s] = res[d * kept:(d + 1) * kept]
        if x == 0:
            pl.semaphore_wait(barrier, n_gy - 1)
        for k, d in enumerate(peers):
            cp = pltpu.make_async_remote_copy(
                src_ref=proj.at[d, x], dst_ref=core.at[x, mine], send_sem=ssem.at[x, k],
                recv_sem=rsem.at[x, k], device_id=(gx, d, gz), device_id_type=MESH,
            )
            cp.start()
            cps.append(cp)
        cp = pltpu.make_async_copy(proj.at[gy, x], core.at[x, mine], lsem.at[x])
        cp.start()
        cps.append(cp)
    row, col, eye = triangles()
    r[...] = started[...]
    nb = r.shape[0] // B
    for step in range(ITERS, nb):
        load_block(step, r, m_g, eye)
        factor_blocks([m_g])
        finish_block(step, r, m_g, row, col)
    scale = 1.0 / jnp.sqrt(F32(columns))
    factor[...] = jnp.zeros_like(factor)
    for i, j in upper(nb):
        @pl.when((gy == j) & (gz == i))
        def _():
            factor[...] = r[i * B:(i + 1) * B, j * B:(j + 1) * B].T * scale
    for cp in cps:
        cp.wait()


def per_device(sizes, field, start_basis):
    n_gx, n_gy, n_gz = sizes
    planes, rows, species, width = field.shape
    n, rank = start_basis.shape
    quarter = species // n_gy
    chunks = planes * quarter
    nb = n // B
    total = len(above(nb)) * B
    columns = planes * n_gx * species * width * n_gz
    n_g = total // 4 // n_gx
    others = 2 * n_gx - 1
    n_sems = 1 + others + (n_gy - 1) + 1 + others + (n_gy - 1) + 2 * (2 * others + 1)
    rows_d = B // (4 * n_gx)
    packed, diagonal, reg = pl.pallas_call(
        functools.partial(gram_kernel, sizes),
        out_shape=(
            jax.ShapeDtypeStruct((total, B), F32),
            jax.ShapeDtypeStruct((n_gy, 4 * n_gx, rows_d, B), F32),
            jax.ShapeDtypeStruct((chunks, n, width), F32),
        ),
        in_specs=[HBM],
        out_specs=(VMEM, VMEM, VMEM),
        scratch_shapes=[
            pltpu.VMEM((total, B), F32),
            pltpu.VMEM((n, n), F32),
            pltpu.VMEM((total // 2, B), F32),
            pltpu.VMEM((2 * n_gx - 1, n_g, B), F32),
            pltpu.VMEM((n_gy - 1, n_g, B), F32),
            pltpu.VMEM((planes * species, rows, width), F32),
            pltpu.VMEM((B, B), F32),
            pltpu.VMEM((4 * n_gx, rows_d, B), F32),
            pltpu.VMEM((2 * n_gx, rows_d, B), F32),
            pltpu.VMEM((others, rows_d, B), F32),
            pltpu.SemaphoreType.DMA((2, n_sems)),
            pltpu.SemaphoreType.DMA((chunks, n_gy - 1)),
            pltpu.SemaphoreType.DMA((chunks, n_gy - 1)),
            pltpu.SemaphoreType.DMA((chunks,)),
            pltpu.SemaphoreType.DMA((planes * species,)),
        ],
        compiler_params=pltpu.CompilerParams(
            collective_id=0, has_side_effects=True, vmem_limit_bytes=32 << 20
        ),
        name="gram",
    )(field)
    basis_t, started = pl.pallas_call(
        basis_kernel,
        out_shape=(
            jax.ShapeDtypeStruct((rank, n), F32),
            jax.ShapeDtypeStruct((n, n), F32),
        ),
        in_specs=[VMEM, VMEM, VMEM],
        out_specs=(VMEM, VMEM),
        scratch_shapes=[
            pltpu.VMEM((n, n), F32),
            pltpu.VMEM((B, 2 * B), F32),
            pltpu.VMEM((B, 2 * B), F32),
        ],
        compiler_params=pltpu.CompilerParams(vmem_limit_bytes=32 << 20),
        name="solve",
    )(packed, diagonal, start_basis)
    core, factor = pl.pallas_call(
        functools.partial(core_kernel, n_gy, columns),
        out_shape=(
            jax.ShapeDtypeStruct((planes, species, rank // n_gy, width), F32),
            jax.ShapeDtypeStruct((n // n_gy, n // n_gz), F32),
        ),
        in_specs=[VMEM, VMEM, VMEM],
        out_specs=(VMEM, VMEM),
        scratch_shapes=[
            pltpu.VMEM((n, n), F32),
            pltpu.VMEM((B, 2 * B), F32),
            pltpu.VMEM((n_gy, planes, quarter, rank // n_gy, width), F32),
            pltpu.SemaphoreType.DMA((planes, n_gy - 1)),
            pltpu.SemaphoreType.DMA((planes, n_gy - 1)),
            pltpu.SemaphoreType.DMA((planes,)),
        ],
        compiler_params=pltpu.CompilerParams(
            collective_id=1, has_side_effects=True, vmem_limit_bytes=32 << 20
        ),
        name="core",
    )(basis_t, reg, started)
    return factor, jnp.transpose(core, (0, 2, 1, 3))


def solution(mesh):
    sizes = tuple(mesh.shape[a] for a in ("gx", "gy", "gz"))
    return jax.shard_map(
        functools.partial(per_device, sizes),
        mesh=mesh,
        in_specs=(P("gx", "gy", None, "gz"), P()),
        out_specs=(P("gy", "gz"), P("gx", "gy", None, "gz")),
        check_vma=False,
    )
```

time: 121 us -> 99.6 us (0.82)
  Pallas kernels: 118 us -> 95.4 us
    pallas_call x2, Pallas kernels: 39.5 us -> 26.3 us  [the longest x1 15.6 us: per_device(): pl.pallas_call(functools.partial(core_kernel, n_gy, columns), out_shape=(...]
    pallas_call x1, Pallas kernels: 78.3 us -> 69.2 us  [per_device(): pl.pallas_call(functools.partial(gram_kernel, sizes), out_shape=(jax.Shap...]
    unnamed x5 -> x6, local copies, waits for them, and re-layouts: 2.69 us -> 3.32 us
where the time goes in v1:
time: 99.6 us; the launch traced here: 99.4 us
  Pallas kernels  95.4 us (96%)
  local copies, waits for them, and re-layouts  3.32 us (3%)
    pallas_call x1, Pallas kernels, per_device(): pl.pallas_call(functools.partial(gram_kernel, sizes), out_shape=(jax.Shap...  69.2 us
    pallas_call x1, Pallas kernels, per_device(): pl.pallas_call(functools.partial(core_kernel, n_gy, columns), out_shape=(...  15.6 us
    pallas_call x1, Pallas kernels, per_device(): pl.pallas_call(basis_kernel, out_shape=(jax.ShapeDtypeStruct((rank, n), F...  10.7 us
    unnamed x6, local copies, waits for them, and re-layouts  3.32 us

profile of v1, /device:TPU:0, one launch (start us, length us, event | category | flops | bytes accessed | tf_op | source)
XLA Modules:
  0.0 99.4 jit_solution(12508127794938001137)
XLA Ops:
  0.6 0.0 copy-start
  0.6 1.6 %copy-done = f32[2,128,16,128]{3,2,1,0:T(8,128)S(1)} copy-done((f32[2,128,16,128]{3,2,1,0:T(8,128)S(1)}, f32[2,128,16,128]{3,2,1,0:T(8,128)}, u32[]{:S(2)}) %copy-start) | copy-done | bytes 2097176
  2.2 0.0 copy-start.1
  2.2 69.2 %gram.1 = (f32[768,128]{1,0:T(8,128)S(1)}, f32[4,8,16,128]{3,2,1,0:T(8,128)S(1)}, f32[8,512,128]{2,1,0:T(8,128)S(1)}) custom-call(f32[2,128,16,128]{3,2,1,0:T(8,128)S(1)} %copy-done), custom_call_target="tpu_custom_call" | custom-call | tf_op jit(solution)/shard_map/gram/pallas_call | solution.py:370
  71.4 0.0 copy-done.1
  71.4 10.7 %solve.1 = (f32[128,512]{1,0:T(8,128)S(1)}, f32[512,512]{1,0:T(8,128)S(1)}) custom-call(f32[768,128]{1,0:T(8,128)S(1)} %get-tuple-element.9.packed, f32[4,8,16,128]{3,2,1,0:T(8,128)S(1)} %get-tuple-element.10.diagonal, f32[512,128]{1,0:T(8,128)S(1)} %copy-done.1), custom_call_target="tpu_custom_call" | custom-call | tf_op jit(solution)/shard_map/solve/pallas_call | solution.py:401
  82.1 15.6 %core.1 = (f32[2,16,32,128]{3,2,1,0:T(8,128)S(1)}, f32[128,128]{1,0:T(8,128)S(1)}) custom-call(f32[128,512]{1,0:T(8,128)S(1)} %get-tuple-element.11.basis_t, f32[8,512,128]{2,1,0:T(8,128)S(1)} %get-tuple-element.12.reg, f32[512,512]{1,0:T(8,128)S(1)} %get-tuple-element.13.started), custom_call_target="tpu_custom_call" | custom-call | tf_op jit(solution)/shard_map/core/pallas_call | solution.py:417
  97.7 1.1 %copy.4 = f32[2,32,16,128]{3,2,1,0:T(8,128)} copy(f32[2,32,16,128]{3,1,2,0:T(8,128)S(1)} %bitcast.1) | data formatting | bytes 1048576
  98.8 0.6 copy.6
Async XLA Ops:
  0.6 1.6 %copy-start = (f32[2,128,16,128]{3,2,1,0:T(8,128)S(1)}, f32[2,128,16,128]{3,2,1,0:T(8,128)}, u32[]{:S(2)}) copy-start(f32[2,128,16,128]{3,2,1,0:T(8,128)} %field.1) | copy-start | bytes 6291460
  2.2 69.2 %copy-start.1 = (f32[512,128]{1,0:T(8,128)S(1)}, f32[512,128]{1,0:T(8,128)}, u32[]{:S(2)}) copy-start(f32[512,128]{1,0:T(8,128)} %start.1) | copy-start | bytes 786436
